TPU v7x, 32 devices: a whole 2x2x4 slice. The times are simulated.
32 devices in a mesh: acq: 4 (over z), line: 8 (over y, x, core).
Axes of the slice: x: 2, y: 2, z: 4, core: 2. Of those that a mesh axis runs over, the one named last changes fastest.
Arguments:
- slc_stack: float32 [2, 64, 64, 512], P(None, 'acq', 'line'), may hold values from -6 to 6
- wavenumbers: float32 [64], replicated, may hold values from -0.8 to 0.8
Outputs:
- spectrum: bfloat16 [256, 64, 512], P(None, 'line', 'acq')
All inputs are finite; a program needn't handle non-finite values.
Results may differ from a plain program's by a relative error of at most 0.001.
Values sent between devices are 32-bit elements; how exact they have to be, the bound alone decides.
A program may use at most 64 MiB of HBM per device.

v0:
```python
import jax
import jax.numpy as jnp
from jax import lax
from jax.sharding import PartitionSpec as P

HEIGHTS = 256
epsilon = 1e-06


def with_line_halo(x, width):
    size, length = (lax.axis_size("line"), x.shape[2])
    up = [(i, i + 1) for i in range(size - 1)]
    down = [(j, i) for i, j in up]
    before = lax.ppermute(x[:, :, length - width :], "line", up)
    after = lax.ppermute(x[:, :, :width], "line", down)
    return jnp.concatenate([before, x, after], axis=2)


def range_halo(x, width):
    parts, acqs, lines, cells = x.shape
    size = lax.axis_size("acq")
    block = cells // size
    padded = jnp.pad(x, ((0, 0), (0, 0), (0, 0), (width, width)))
    edges = []
    for d in range(size):
        left = padded[..., d * block : d * block + width]
        start = (d + 1) * block + width
        right = padded[..., start : start + width]
        edges.append(jnp.concatenate([left, right], axis=3))
    sent = jnp.stack(edges).reshape(size, parts * acqs, lines * 2 * width)
    got = lax.all_to_all(sent, "acq", split_axis=0, concat_axis=0, tiled=True)
    got = got.reshape(size, parts, acqs, lines, 2 * width).transpose(1, 0, 2, 3, 4)
    return got.reshape(parts, size * acqs, lines, 2 * width)


def steering(wavenumbers, count):
    heights = jnp.arange(count, dtype=jnp.int32).astype(jnp.float32) - jnp.float32(count // 2)
    phases = wavenumbers[:, None] * heights[None, :]
    cosine_part = jnp.cos(phases).T
    sine_part = jnp.sin(phases).T
    upper = jnp.concatenate([cosine_part, sine_part], axis=1)
    lower = jnp.concatenate([-sine_part, cosine_part], axis=1)
    return jnp.concatenate([upper, lower], axis=0)


def beamform(stack_block, matrix, count):
    channels = stack_block.shape[0] * stack_block.shape[1]
    flat = stack_block.reshape(channels, -1)
    beams = jnp.dot(matrix, flat, precision=lax.Precision.HIGH, preferred_element_type=jnp.float32)
    beam_power = beams[:count] * beams[:count] + beams[count:] * beams[count:]
    energy = jnp.sum(flat * flat, axis=0)
    shape = stack_block.shape[2:]
    return (beam_power.reshape((count,) + shape), energy.reshape((1,) + shape))


def sum_range(field, count):
    total = field[..., 0:count]
    for offset in range(1, 7):
        total = total + field[..., offset : offset + count]
    return total


def sum_lines(field, count):
    total = field[..., 0:count, :]
    for offset in range(1, 7):
        total = total + field[..., offset : offset + count, :]
    return total


def body(slc_stack, wavenumbers):
    width = 3
    line_count = slc_stack.shape[2]
    tall = with_line_halo(slc_stack, width)
    edge = range_halo(tall, width)
    regrouped = lax.all_to_all(tall, "acq", split_axis=3, concat_axis=1, tiled=True)
    range_count = regrouped.shape[3]
    matrix = steering(wavenumbers, HEIGHTS)
    inner = beamform(regrouped, matrix, HEIGHTS)
    outer = beamform(edge, matrix, HEIGHTS)
    boxes = []
    for mid, rim in zip(inner, outer):
        mid, rim = (sum_lines(mid, line_count), sum_lines(rim, line_count))
        wide = jnp.concatenate([rim[..., :width], mid, rim[..., width:]], axis=-1)
        boxes.append(sum_range(wide, range_count))
    return (boxes[0] / (boxes[1] + epsilon)).astype(jnp.bfloat16)


def solution(mesh):
    placed = (P(None, "acq", "line", None), P())
    return jax.shard_map(
        body, mesh=mesh, in_specs=placed, out_specs=P(None, "line", "acq"), check_vma=False
    )
```

profile of v0, /device:TPU:0, one launch (start us, length us, event | category | flops | bytes accessed | tf_op | source)
XLA Modules:
  0.0 129.8 jit_solution(5151484903050266016)
XLA Ops:
  0.0 1.4 %fusion.34 = (f32[2,16,3,512]{3,2,1,0:T(4,128)S(1)}, f32[2,16,3,512]{3,2,1,0:T(4,128)S(1)}) fusion(f32[2,16,8,512]{3,2,1,0:T(8,128)} %param.2), kind=kLoop, calls=%fused_computation.87 | loop fusion | bytes 786432 | tf_op jit(solution)/shard_map/slice | solution.py:14
  1.5 2.4 %collective-permute-start = (f32[2,16,3,512]{3,1,2,0:T(8,128)S(1)}, f32[2,16,3,512]{3,1,2,0:T(8,128)S(1)}, u32[]{:S(2)}, u32[]{:S(2)}) collective-permute-start(f32[2,16,3,512]{3,1,2,0:T(8,128)S(1)} %copy.95), channel_id=1, source_target_pairs={{0,1},{1,2},{2,3},{3,4},{4,5},{5,6},{6,7},{8,9},{9,10},{10,11},{11... | collective-permute-start | bytes 589832 | tf_op jit(solution)/shard_map/ppermute | solution.py:14
  4.0 1.3 collective-permute-start.1
  5.3 8.2 %copy.75 = f32[2,16,8,512]{2,1,0,3:T(8,128)} copy(f32[2,16,8,512]{3,2,1,0:T(8,128)} %param.2) | data formatting | bytes 1048576 | tf_op args[0]
  13.5 0.5 multiply_sine_fusion
  14.1 7.5 %copy.74 = f32[2,16,3,512]{2,1,0,3:T(8,128)} copy(f32[2,16,3,512]{3,1,2,0:T(8,128)S(1)} %collective-permute-done) | data formatting | bytes 393216 | tf_op jit(solution)/shard_map/ppermute | solution.py:14
  21.6 7.5 %copy.76 = f32[2,16,3,512]{2,1,0,3:T(8,128)} copy(f32[2,16,3,512]{3,1,2,0:T(8,128)S(1)} %collective-permute-done.1) | data formatting | bytes 393216 | tf_op jit(solution)/shard_map/ppermute | solution.py:15
  29.1 10.5 %pad_maximum_fusion = f32[2,16,14,512]{2,1,0,3:T(8,128)S(1)} fusion(f32[2,16,3,512]{2,1,0,3:T(8,128)} %copy.76, f32[2,16,8,512]{2,1,0,3:T(8,128)} %copy.75, f32[2,16,3,512]{2,1,0,3:T(8,128)} %copy.74), kind=kLoop, calls=%fused_computation | loop fusion | flops 458752 | bytes 1835008 | tf_op jit(solution)/shard_map/concatenate | solution.py:16
  39.6 0.2 copy.78
  40.0 0.2 copy.79
  41.0 0.6 pad_maximum_fusion.5
  41.7 5.7 %all-to-all-start = ((f32[4,32,84]{2,1,0:T(8,128)}), f32[4,32,84]{2,1,0:T(8,128)S(1)}, u32[]{:S(2)}, u32[]{:S(2)}) async-start(f32[4,32,84]{2,1,0:T(8,128)} %pad_maximum_fusion.5), calls=%async_computation | async-start | bytes 131072 | tf_op jit(solution)/shard_map/all_to_all | solution.py:31
  47.4 13.2 %fusion.38 = f32[512,2,16,14]{3,2,1,0:T(8,128)} fusion(f32[2,16,3,512]{2,1,0,3:T(8,128)} %copy.76, f32[2,16,8,512]{2,1,0,3:T(8,128)} %copy.75, f32[2,16,3,512]{2,1,0,3:T(8,128)} %copy.74), kind=kLoop, calls=%fused_computation.90 | loop fusion | flops 458752 | bytes 1835008
  60.6 10.1 %reshape.44 = f32[4,1,57344]{2,1,0:T(1,128)} reshape(f32[512,2,16,14]{3,2,1,0:T(8,128)} %fusion.38) | data formatting | bytes 1835008
  70.7 5.1 %all-to-all-start.1 = ((f32[4,1,57344]{2,1,0:T(1,128)}), f32[4,1,57344]{2,1,0:T(1,128)S(1)}, u32[]{:S(2)}, u32[]{:S(2)}) async-start(f32[4,1,57344]{2,1,0:T(1,128)} %reshape.44), calls=%async_computation.1 | async-start | bytes 1835008 | tf_op jit(solution)/shard_map/all_to_all | solution.py:75
  75.9 0.2 reshape.38
  76.2 0.3 multiply_reduce_fusion.1
  77.0 0.2 reshape_reshape.3
  77.2 0.4 fusion.17
  77.7 21.9 %all-to-all-done.1 = f32[4,1,57344]{2,1,0:T(1,128)S(1)} async-done(((f32[4,1,57344]{2,1,0:T(1,128)}), f32[4,1,57344]{2,1,0:T(1,128)S(1)}, u32[]{:S(2)}, u32[]{:S(2)}) %all-to-all-start.1) | async-done | bytes 917536 | tf_op jit(solution)/shard_map/all_to_all | solution.py:75
  99.6 0.5 broadcast.20
  100.1 3.3 %reduce.2 = f32[4,57344]{1,0:T(4,128)S(1)} reduce(f32[4,1,57344]{2,1,0:T(1,128)S(1)} %all-to-all-done.1, f32[]{:T(128)} %broadcast.20), dimensions={1}, to_apply=%all_to_all.15.reduce_sub_computation | reduce | bytes 1835012 | tf_op jit(solution)/shard_map/all_to_all | solution.py:75
  103.4 12.7 %reshape.45 = f32[512,2,16,14]{3,2,1,0:T(8,128)} reshape(f32[4,57344]{1,0:T(4,128)S(1)} %reduce.2) | data formatting | bytes 1835008
  116.1 5.7 %copy.94 = f32[2,16,14,4,128]{4,3,1,2,0:T(4,128)S(1)} copy(f32[2,16,14,4,128]{2,1,0,4,3:T(8,128)} %bitcast.34) | data formatting | bytes 1835008 | tf_op jit(solution)/shard_map/all_to_all | solution.py:75
  121.7 0.2 multiply_reduce_fusion
  122.0 0.5 copy.88
  122.5 1.8 %fusion.13 = f32[512,1792]{1,0:T(8,128)S(1)} fusion(f32[16,8,14,128]{3,2,1,0:T(8,128)S(1)} %bitcast.36, f32[256,64]{1,0:T(8,128)S(1)} %get-tuple-element.19, f32[256,64]{1,0:T(8,128)S(1)} %get-tuple-element.18, f32[256,64]{1,0:T(8,128)S(1)} %get-tuple-element.17), kind=kOutput, calls=%fused_computation.32 | convolution fusion | flops 704839680 | bytes 4784128 | tf_op jit(solution)/shard_map/dot_general | solution.py:49
  124.3 1.5 %fusion = f32[256,1792]{1,0:T(8,128)} fusion(f32[512,1792]{1,0:T(8,128)S(1)} %fusion.13), kind=kLoop, calls=%fused_computation.2 | loop fusion | flops 1376256 | bytes 5505024 | tf_op jit(solution)/shard_map/add | solution.py:50
  125.7 1.8 %copy.89 = f32[256,1792]{0,1:T(8,128)S(1)} copy(f32[256,1792]{1,0:T(8,128)} %fusion) | data formatting | bytes 3670016 | tf_op jit(solution)/shard_map/add | solution.py:50
  127.6 0.2 slice_add_fusion
  127.9 0.9 fusion.12
  128.8 1.1 copy.93
  (35 shorter events, 1.9 us)
Async XLA Ops:
  0.0 13.5 %copy-start = (f32[64]{0:T(128)S(1)}, f32[64]{0:T(128)}, u32[]{:S(2)}) copy-start(f32[64]{0:T(128)} %param.3) | copy-start | bytes 772
  1.5 12.6 %collective-permute-start = (f32[2,16,3,512]{3,1,2,0:T(8,128)S(1)}, f32[2,16,3,512]{3,1,2,0:T(8,128)S(1)}, u32[]{:S(2)}, u32[]{:S(2)}) collective-permute-start(f32[2,16,3,512]{3,1,2,0:T(8,128)S(1)} %copy.95), channel_id=1, source_target_pairs={{0,1},{1,2},{2,3},{3,4},{4,5},{5,6},{6,7},{8,9},{9,10},{10,11},{11... | collective-permute-start | bytes 589832 | tf_op jit(solution)/shard_map/ppermute | solution.py:14
  4.0 17.6 %collective-permute-start.1 = (f32[2,16,3,512]{3,1,2,0:T(8,128)S(1)}, f32[2,16,3,512]{3,1,2,0:T(8,128)S(1)}, u32[]{:S(2)}, u32[]{:S(2)}) collective-permute-start(f32[2,16,3,512]{3,1,2,0:T(8,128)S(1)} %copy.96), channel_id=1, source_target_pairs={{1,0},{2,1},{3,2},{4,3},{5,4},{6,5},{7,6},{9,8},{10,9},{11,10},{12... | collective-permute-start | bytes 589832 | tf_op jit(solution)/shard_map/ppermute | solution.py:15
  41.7 29.0 %all-to-all-start = ((f32[4,32,84]{2,1,0:T(8,128)}), f32[4,32,84]{2,1,0:T(8,128)S(1)}, u32[]{:S(2)}, u32[]{:S(2)}) async-start(f32[4,32,84]{2,1,0:T(8,128)} %pad_maximum_fusion.5), calls=%async_computation | async-start | bytes 131072 | tf_op jit(solution)/shard_map/all_to_all | solution.py:31
  70.7 28.8 %all-to-all-start.1 = ((f32[4,1,57344]{2,1,0:T(1,128)}), f32[4,1,57344]{2,1,0:T(1,128)S(1)}, u32[]{:S(2)}, u32[]{:S(2)}) async-start(f32[4,1,57344]{2,1,0:T(1,128)} %reshape.44), calls=%async_computation.1 | async-start | bytes 1835008 | tf_op jit(solution)/shard_map/all_to_all | solution.py:75
where the time goes:
time: 130 us
  local copies, waits for them, and re-layouts  59.6 us (46%)
  other arithmetic  31.5 us (24%)
  waiting for transfers between devices  21.9 us (17%)
  starting transfers between devices  14.5 us (11%)
  matrix products  2.13 us (2%)
    unnamed x9, local copies, waits for them, and re-layouts  31.4 us
    all_to_all x1, waiting for transfers between devices, body(): lax.all_to_all(tall, 'acq', split_axis=3, concat_axis=1, tiled=True)  21.9 us
    unnamed x1, other arithmetic  13.2 us
    concatenate x1, other arithmetic, with_line_halo(): return jnp.concatenate([before, x, after], axis=2)  10.5 us
    ppermute x1, local copies, waits for them, and re-layouts, with_line_halo(): before = lax.ppermute(x[:, :, length - width:], 'line', up)  7.51 us
    ppermute x1, local copies, waits for them, and re-layouts, with_line_halo(): after = lax.ppermute(x[:, :, :width], 'line', down)  7.5 us
    all_to_all x3, local copies, waits for them, and re-layouts, body(): lax.all_to_all(tall, 'acq', split_axis=3, concat_axis=1, tiled=True)  6.72 us
    all_to_all x1, starting transfers between devices, range_halo(): got = lax.all_to_all(sent, 'acq', split_axis=0, concat_axis=0, tiled=True)  5.69 us
  transfers between devices with their start and end apart: 4, of which 1 were waited for; matrix products, arithmetic and copies ran while one was open for 32% of the time, Pallas kernels for 0%

commit v1 on v0

--- a/solution.py
+++ b/solution.py
@@ -72,7 +72,15 @@
     line_count = slc_stack.shape[2]
     tall = with_line_halo(slc_stack, width)
     edge = range_halo(tall, width)
-    regrouped = lax.all_to_all(tall, "acq", split_axis=3, concat_axis=1, tiled=True)
+
+    def _note_point(piece_in, mesh_dim):
+        block_now = jnp.split(piece_in, lax.axis_size(mesh_dim), axis=3)
+        field_out = jnp.stack(block_now)
+        base_arr = lax.all_to_all(field_out, concat_axis=0, axis_name=mesh_dim, split_axis=0)
+        back = jnp.concatenate(base_arr, axis=1)
+        return back
+
+    regrouped = _note_point(tall, "acq")
     range_count = regrouped.shape[3]
     matrix = steering(wavenumbers, HEIGHTS)
     inner = beamform(regrouped, matrix, HEIGHTS)

time: 130 us -> 59.8 us (0.46)
  the two profiles are of different devices: /device:TPU:0 before, /device:TPU:3 now
where the time goes in v1:
time: 59.8 us; the launch traced here: 59.4 us
  waiting for transfers between devices  29.7 us (50%)
  starting transfers between devices  13.7 us (23%)
  local copies, waits for them, and re-layouts  8.1 us (14%)
  other arithmetic  5.59 us (9%)
  matrix products  2.13 us (4%)
    all_to_all x1, waiting for transfers between devices, _note_point(): lax.all_to_all(field_out, concat_axis=0, axis_name=mesh_dim, split_axis=0)  21.1 us
    ppermute x1, waiting for transfers between devices, with_line_halo(): after = lax.ppermute(x[:, :, :width], 'line', down)  5.02 us
    all_to_all x1, starting transfers between devices, range_halo(): got = lax.all_to_all(sent, 'acq', split_axis=0, concat_axis=0, tiled=True)  4.59 us
    ppermute x1, starting transfers between devices, with_line_halo(): before = lax.ppermute(x[:, :, length - width:], 'line', up)  3.68 us
    all_to_all x1, waiting for transfers between devices, range_halo(): got = lax.all_to_all(sent, 'acq', split_axis=0, concat_axis=0, tiled=True)  3.56 us
    all_to_all x1, starting transfers between devices, _note_point(): lax.all_to_all(field_out, concat_axis=0, axis_name=mesh_dim, split_axis=0)  3.5 us
    dot_general x2, matrix products, beamform(): jnp.dot(matrix, flat, precision=lax.Precision.HIGH, preferred_element_typ...  2.13 us
    ppermute x1, starting transfers between devices, with_line_halo(): after = lax.ppermute(x[:, :, :width], 'line', down)  1.92 us
  transfers between devices with their start and end apart: 4, of which 3 were waited for; matrix products, arithmetic and copies ran while one was open for 6% of the time, Pallas kernels for 0%

profile of v1, /device:TPU:3, one launch (start us, length us, event | category | flops | bytes accessed | tf_op | source)
XLA Modules:
  0.0 59.4 jit_solution(10643331105282558041)
XLA Ops:
  0.0 1.4 %fusion.34 = (f32[2,16,3,512]{3,2,1,0:T(4,128)S(1)}, f32[2,16,3,512]{3,2,1,0:T(4,128)S(1)}) fusion(f32[2,16,8,512]{3,2,1,0:T(8,128)} %param.2), kind=kLoop, calls=%fused_computation.94 | loop fusion | bytes 786432 | tf_op jit(solution)/shard_map/slice | solution.py:15
  1.5 3.7 %collective-permute-start = (f32[2,16,3,512]{3,1,2,0:T(8,128)S(1)}, f32[2,16,3,512]{3,1,2,0:T(8,128)S(1)}, u32[]{:S(2)}, u32[]{:S(2)}) collective-permute-start(f32[2,16,3,512]{3,1,2,0:T(8,128)S(1)} %copy.72), channel_id=1, source_target_pairs={{0,1},{1,2},{2,3},{3,4},{4,5},{5,6},{6,7},{8,9},{9,10},{10,11},{11... | collective-permute-start | bytes 589832 | tf_op jit(solution)/shard_map/ppermute | solution.py:14
  5.2 1.9 %collective-permute-start.1 = (f32[2,16,3,512]{3,1,2,0:T(8,128)S(1)}, f32[2,16,3,512]{3,1,2,0:T(8,128)S(1)}, u32[]{:S(2)}, u32[]{:S(2)}) collective-permute-start(f32[2,16,3,512]{3,1,2,0:T(8,128)S(1)} %copy.73), channel_id=1, source_target_pairs={{1,0},{2,1},{3,2},{4,3},{5,4},{6,5},{7,6},{9,8},{10,9},{11,10},{12... | collective-permute-start | bytes 589832 | tf_op jit(solution)/shard_map/ppermute | solution.py:15
  7.2 0.5 multiply_sine_fusion
  7.8 0.3 constant_dynamic-update-slice_fusion.1
  8.1 5.0 %collective-permute-done.1 = f32[2,16,3,512]{3,1,2,0:T(8,128)S(1)} collective-permute-done((f32[2,16,3,512]{3,1,2,0:T(8,128)S(1)}, f32[2,16,3,512]{3,1,2,0:T(8,128)S(1)}, u32[]{:S(2)}, u32[]{:S(2)}) %collective-permute-start.1) | collective-permute-done | bytes 196640 | tf_op jit(solution)/shard_map/ppermute | solution.py:15
  13.2 0.3 fusion.33
  13.5 0.2 copy.64
  13.9 0.2 copy.65
  14.4 0.2 pad_maximum_fusion.3
  14.6 0.2 copy.49
  14.8 0.1 stack.31
  15.0 0.2 copy.50
  15.3 0.1 stack.32
  15.5 0.6 %pad_maximum_fusion.5 = f32[4,32,84]{2,1,0:T(8,128)} fusion(f32[1,32,84]{2,1,0:T(8,128)S(1)} %copy.55, f32[1,32,84]{2,1,0:T(8,128)S(1)} %copy.54, f32[1,32,84]{2,1,0:T(8,128)S(1)} %copy.53, f32[1,32,84]{2,1,0:T(8,128)S(1)} %copy.52), kind=kLoop, calls=%fused_computation.56 | loop fusion | flops 32256 | bytes 86016 | tf_op jit(solution)/shard_map/stack | solution.py:30
  16.1 4.6 %all-to-all-start = ((f32[4,32,84]{2,1,0:T(8,128)}), f32[4,32,84]{2,1,0:T(8,128)S(1)}, u32[]{:S(2)}, u32[]{:S(2)}) async-start(f32[4,32,84]{2,1,0:T(8,128)} %pad_maximum_fusion.5), calls=%async_computation | async-start | bytes 131072 | tf_op jit(solution)/shard_map/all_to_all | solution.py:31
  20.7 1.0 %pad_maximum_fusion.2 = f32[4,2,16,14,128]{4,2,3,1,0:T(8,128)} fusion(f32[1,2,16,14,128]{4,2,3,1,0:T(8,128)S(1)} %get-tuple-element.6, f32[1,2,16,14,128]{4,2,3,1,0:T(8,128)S(1)} %get-tuple-element.7, f32[1,2,16,14,128]{4,2,3,1,0:T(8,128)S(1)} %get-tuple-element.8, f32[1,2,16,14,128]{4,2,3,1,0:T(8,128)S(1)} %get-tuple-element.5), kind=kLoop, calls=%fused_computation.34 | loop fusion | flops 688128 | bytes 1835008 | tf_op jit(solution)/shard_map/stack | solution.py:78
  21.7 3.6 %all-to-all-done = f32[4,32,84]{2,1,0:T(8,128)S(1)} async-done(((f32[4,32,84]{2,1,0:T(8,128)}), f32[4,32,84]{2,1,0:T(8,128)S(1)}, u32[]{:S(2)}, u32[]{:S(2)}) %all-to-all-start) | async-done | bytes 43040 | tf_op jit(solution)/shard_map/all_to_all | solution.py:31
  25.3 3.5 %all-to-all-start.1 = ((f32[4,2,16,14,128]{4,2,3,1,0:T(8,128)}), f32[4,2,16,14,128]{4,2,3,1,0:T(8,128)S(1)}, u32[]{:S(2)}, u32[]{:S(2)}) async-start(f32[4,2,16,14,128]{4,2,3,1,0:T(8,128)} %pad_maximum_fusion.2), calls=%async_computation.1 | async-start | bytes 1835008 | tf_op jit(solution)/shard_map/all_to_all | solution.py:79
  28.8 0.1 copy.56
  28.9 0.2 reshape.37
  29.2 0.3 multiply_reduce_fusion.1
  30.0 0.2 reshape_reshape.6
  30.2 0.4 fusion.17
  30.7 21.1 %all-to-all-done.1 = f32[4,2,16,14,128]{4,2,3,1,0:T(8,128)S(1)} async-done(((f32[4,2,16,14,128]{4,2,3,1,0:T(8,128)}), f32[4,2,16,14,128]{4,2,3,1,0:T(8,128)S(1)}, u32[]{:S(2)}, u32[]{:S(2)}) %all-to-all-start.1) | async-done | bytes 917536 | tf_op jit(solution)/shard_map/all_to_all | solution.py:79
  51.8 0.3 copy.58
  52.1 1.8 %fusion.13 = f32[512,1792]{1,0:T(8,128)S(1)} fusion(f32[16,8,14,128]{3,2,1,0:T(8,128)S(1)} %bitcast.39, f32[256,64]{1,0:T(8,128)S(1)} %get-tuple-element.23, f32[256,64]{1,0:T(8,128)S(1)} %get-tuple-element.22, f32[256,64]{1,0:T(8,128)S(1)} %get-tuple-element.21), kind=kOutput, calls=%fused_computation.31 | convolution fusion | flops 704839680 | bytes 4784128 | tf_op jit(solution)/shard_map/dot_general | solution.py:49
  53.9 1.4 %fusion = f32[256,1792]{1,0:T(8,128)} fusion(f32[512,1792]{1,0:T(8,128)S(1)} %fusion.13), kind=kLoop, calls=%fused_computation.1 | loop fusion | flops 1376256 | bytes 5505024 | tf_op jit(solution)/shard_map/add | solution.py:50
  55.3 1.8 %copy.59 = f32[256,1792]{0,1:T(8,128)S(1)} copy(f32[256,1792]{1,0:T(8,128)} %fusion) | data formatting | bytes 3670016 | tf_op jit(solution)/shard_map/add | solution.py:50
  57.1 0.2 slice_add_fusion
  57.5 0.9 %fusion.12 = bf16[256,8,128]{0,2,1:T(8,128)(2,1)S(1)} fusion(f32[256,8,3]{0,2,1:T(4,128)S(1)} %get-tuple-element.18, f32[256,8,128]{0,2,1:T(8,128)S(1)} %slice_add_fusion, f32[256,8,3]{0,2,1:T(4,128)S(1)} %get-tuple-element.17, f32[8,128]{1,0:T(8,128)S(1)} %fusion.23), kind=kLoop, calls=%fused_computation.30 | loop fusion | flops 3670016 | bytes 1626112 | tf_op jit(solution)/shard_map/convert_element_type | solution.py:93
  58.3 1.1 %copy.63 = bf16[256,8,128]{2,1,0:T(8,128)(2,1)} copy(bf16[256,8,128]{0,2,1:T(8,128)(2,1)S(1)} %fusion.12) | data formatting | bytes 1048576 | tf_op jit(solution)/shard_map/convert_element_type | solution.py:93
  (32 shorter events, 1.5 us)
Async XLA Ops:
  0.0 7.8 %copy-start = (f32[2,16,8,512]{3,2,1,0:T(8,128)S(1)}, f32[2,16,8,512]{3,2,1,0:T(8,128)}, u32[]{:S(2)}) copy-start(f32[2,16,8,512]{3,2,1,0:T(8,128)} %param.2) | copy-start | bytes 1572868
  0.0 7.2 %copy-start.1 = (f32[64]{0:T(128)S(1)}, f32[64]{0:T(128)}, u32[]{:S(2)}) copy-start(f32[64]{0:T(128)} %param.3) | copy-start | bytes 772
  1.5 6.3 %collective-permute-start = (f32[2,16,3,512]{3,1,2,0:T(8,128)S(1)}, f32[2,16,3,512]{3,1,2,0:T(8,128)S(1)}, u32[]{:S(2)}, u32[]{:S(2)}) collective-permute-start(f32[2,16,3,512]{3,1,2,0:T(8,128)S(1)} %copy.72), channel_id=1, source_target_pairs={{0,1},{1,2},{2,3},{3,4},{4,5},{5,6},{6,7},{8,9},{9,10},{10,11},{11... | collective-permute-start | bytes 589832 | tf_op jit(solution)/shard_map/ppermute | solution.py:14
  5.2 7.9 %collective-permute-start.1 = (f32[2,16,3,512]{3,1,2,0:T(8,128)S(1)}, f32[2,16,3,512]{3,1,2,0:T(8,128)S(1)}, u32[]{:S(2)}, u32[]{:S(2)}) collective-permute-start(f32[2,16,3,512]{3,1,2,0:T(8,128)S(1)} %copy.73), channel_id=1, source_target_pairs={{1,0},{2,1},{3,2},{4,3},{5,4},{6,5},{7,6},{9,8},{10,9},{11,10},{12... | collective-permute-start | bytes 589832 | tf_op jit(solution)/shard_map/ppermute | solution.py:15
  16.1 9.2 %all-to-all-start = ((f32[4,32,84]{2,1,0:T(8,128)}), f32[4,32,84]{2,1,0:T(8,128)S(1)}, u32[]{:S(2)}, u32[]{:S(2)}) async-start(f32[4,32,84]{2,1,0:T(8,128)} %pad_maximum_fusion.5), calls=%async_computation | async-start | bytes 131072 | tf_op jit(solution)/shard_map/all_to_all | solution.py:31
  25.3 26.4 %all-to-all-start.1 = ((f32[4,2,16,14,128]{4,2,3,1,0:T(8,128)}), f32[4,2,16,14,128]{4,2,3,1,0:T(8,128)S(1)}, u32[]{:S(2)}, u32[]{:S(2)}) async-start(f32[4,2,16,14,128]{4,2,3,1,0:T(8,128)} %pad_maximum_fusion.2), calls=%async_computation.1 | async-start | bytes 1835008 | tf_op jit(solution)/shard_map/all_to_all | solution.py:79
